TPU v7x, 32 devices: a whole 2x2x4 slice. The times are simulated.
32 devices in a mesh: gx: 8 (over z, y), gy: 4 (over x, core).
Axes of the slice: x: 2, y: 2, z: 4, core: 2. Of those that a mesh axis runs over, the one named last changes fastest.
Arguments:
- right_side: float32 [7, 7, 7, 16, 16, 128], P(None, None, None, 'gx', 'gy'), may hold values from -6 to 6
- coefficient: float32 [16, 16, 128], P('gx', 'gy'), may hold values from 0.2 to 5
- degrees: int32 [3, 16, 16, 128], P(None, 'gx', 'gy'), may hold values from 2 to 6
Outputs:
- smoothed: float32 [7, 7, 7, 16, 16, 128], P(None, None, None, 'gx', 'gy')
- coarse_residual: float32 [64, 16, 2048], P(None, 'gx', 'gy')
All inputs are finite; a program needn't handle non-finite values.
Results may differ from a plain program's by a relative error of at most 0.0003.
Values sent between devices are 32-bit elements; how exact they have to be, the bound alone decides.
A program may use at most 64 MiB of HBM per device.

v0:
```python
import functools

import jax
import jax.numpy as jnp
from jax import lax
from jax.experimental import pallas as pl
from jax.experimental.pallas import tpu as pltpu
from jax.sharding import PartitionSpec as P

CMODES = 4
LAM_HIGH = 6.0
LAM_LOW = 0.5
MODES = 7
MESH = pl.DeviceIdType.MESH
F32 = jnp.float32
HALF = [(2.0 * n + 1.0) / 2.0 for n in range(MODES)]
SLOPE = [n * (n + 1.0) / 2.0 for n in range(MODES)]


def chebyshev():
    centre = (LAM_HIGH + LAM_LOW) / 2.0
    radius = (LAM_HIGH - LAM_LOW) / 2.0
    ratio = centre / radius
    rho = 1.0 / ratio
    pairs = []
    for _ in range(2):
        following = 1.0 / (2.0 * ratio - rho)
        pairs.append((following * rho, 2.0 * following / radius))
        rho = following
    return 1.0 / centre, pairs


def rows(shape):
    return lax.broadcasted_iota(jnp.int32, shape, len(shape) - 2)


def lanes(shape):
    return lax.broadcasted_iota(jnp.int32, shape, len(shape) - 1)


def turn(v, shift):
    return pltpu.roll(v, shift, v.ndim - 2)


def pack_x_up(p, q):
    return jnp.where(rows(p.shape) < 4, turn(p, 4), q)


def pack_x_down(p, q):
    return jnp.where(rows(p.shape) < 4, p, turn(q, 4))


def prev_x(p, q, g):
    low = rows(p.shape) < 4
    return jnp.where(low, g, turn(p, 4)), turn(jnp.where(low, q, g), 4)


def next_x(p, q, g):
    low = rows(p.shape) < 4
    return turn(jnp.where(low, g, p), 4), jnp.where(low, turn(q, 4), g)


def pack_y_up(p, q):
    return jnp.where((rows(p.shape) & 3) == 0, turn(p, 5), turn(q, 6))


def pack_y_down(p, q):
    return jnp.where((rows(p.shape) & 3) == 3, turn(p, 3), turn(q, 2))


def prev_y(p, q, g):
    edge = (rows(p.shape) & 3) == 0
    return jnp.where(edge, g, turn(p, 1)), jnp.where(edge, turn(g, 7), turn(q, 1))


def next_y(p, q, g):
    edge = (rows(p.shape) & 3) == 3
    return jnp.where(edge, g, turn(p, 7)), jnp.where(edge, turn(g, 1), turn(q, 7))


def prev_z(p):
    return jnp.where(lanes(p.shape) == 0, 0.0, pltpu.roll(p, 1, p.ndim - 1))


def next_z(p):
    end = p.shape[-1] - 1
    return jnp.where(lanes(p.shape) == end, 0.0, pltpu.roll(p, end, p.ndim - 1))


def line(u, half_coef):
    t4 = u[4] + u[6]
    t2 = u[2] + t4
    even = u[0] + t2
    t3 = u[3] + u[5]
    odd = u[1] + t3
    s2 = 6.0 * t2
    s4 = s2 + 14.0 * t4
    s6 = s4 + 22.0 * u[6]
    s1 = 2.0 * odd
    s3 = s1 + 10.0 * t3
    s5 = s3 + 18.0 * u[5]
    tp = even + odd
    tm = even - odd
    fp = half_coef * (s6 + s5)
    fm = half_coef * (s5 - s6)
    return (tp, tm, fp, fm), (None, s1, s2, s3, s4, s5, s6)


def spread(traces, before, after, geom, coef, sums, count):
    tp, tm, fp, fm = traces
    tau_a, tau_b, w_a, w_b, k_a, k_b = geom
    jump_a = tp - after[0]
    g_a = tau_a * jump_a - w_a * (fp + after[1])
    jump_b = before[0] - tm
    g_b = tau_b * jump_b - w_b * (before[1] + fm)
    kl = k_a * jump_a
    kr = k_b * jump_b
    p = (g_a - g_b, g_a + g_b)
    q = (kl - kr, kl + kr)
    out = [HALF[0] * p[0]]
    for n in range(1, count):
        out.append(HALF[n] * (coef * sums[n] + (p[n % 2] - SLOPE[n] * q[n % 2])))
    return out


def kernel(nx, ny, rhs, coef, deg, u, coarse, s, inv, step, acc, geo, dia, zm,
           ps, pg, xs, xg, ys, yg, xs3, xg3, ys3, yg3,
           p_send, p_recv, x_send, x_recv, y_send, y_recv):
    gx, gy = lax.axis_index("gx"), lax.axis_index("gy")
    exists = (gx < nx - 1, gx > 0, gy < ny - 1, gy > 0)
    target = ({"gx": gx + 1}, {"gx": gx - 1}, {"gy": gy + 1}, {"gy": gy - 1})
    source = (exists[1], exists[0], exists[3], exists[2])

    barrier = pltpu.get_barrier_semaphore()
    for d in range(4):
        @pl.when(exists[d])
        def _(d=d):
            pl.semaphore_signal(barrier, inc=1, device_id=target[d], device_id_type=MESH)

    def copy(src, dst, send, recv, d):
        return pltpu.make_async_remote_copy(src_ref=src, dst_ref=dst, send_sem=send, recv_sem=recv,
                                            device_id=target[d], device_id_type=MESH)

    def param_copy(d):
        return copy(ps.at[d], pg.at[d], p_send.at[d], p_recv.at[d], d)

    def x_copy(k, d, b):
        if k < 2:
            return copy(xs.at[k, d, b], xg.at[k, d, b], x_send.at[k, d, b], x_recv.at[k, d, b], d)
        return copy(xs3.at[d, b], xg3.at[d, b], x_send.at[k, d, b], x_recv.at[k, d, b], d)

    def y_copy(k, d, a):
        if k < 2:
            return copy(ys.at[k, d, a], yg.at[k, d, a], y_send.at[k, d, a], y_recv.at[k, d, a], 2 + d)
        return copy(ys3.at[d, a], yg3.at[d, a], y_send.at[k, d, a], y_recv.at[k, d, a], 2 + d)

    c = coef[...]
    half_coef = 0.5 * c
    df = [deg[d].astype(F32) for d in range(3)]
    ps[0] = pack_x_up(c, df[0])
    ps[1] = pack_x_down(c, df[0])
    ps[2] = pack_y_up(c, df[1])
    ps[3] = pack_y_down(c, df[1])
    pl.semaphore_wait(barrier, sum(e.astype(jnp.int32) for e in exists))
    for d in range(4):
        @pl.when(exists[d])
        def _(d=d):
            param_copy(d).start()

    for d in range(4):
        @pl.when(jnp.logical_not(source[d]))
        def _(d=d):
            pg[d] = jnp.zeros((8, 128), F32)
            ghosts = (xg, yg)[d // 2]
            ghosts3 = (xg3, yg3)[d // 2]

            def clear(i, _):
                for k in range(2):
                    ghosts[k, d % 2, i] = jnp.zeros((MODES, 8, 128), F32)
                return 0
            lax.fori_loop(0, MODES, clear, 0)

            def clear3(i, _):
                ghosts3[d % 2, i] = jnp.zeros((CMODES, 8, 128), F32)
                return 0
            lax.fori_loop(0, CMODES, clear3, 0)

    shape = (MODES, 8, 128)
    levels = lax.broadcasted_iota(jnp.int32, shape, 0)
    zm[...] = jnp.where(levels <= deg[2][None], 1.0, 0.0)

    def prepare(direction, before, after, first, last):
        degree = df[direction]
        wide_a = jnp.maximum(degree, after[1])
        wide_b = jnp.maximum(degree, before[1])
        tau_a = jnp.maximum(c, after[0]) * (wide_a + 1.0) * (wide_a + 2.0)
        tau_b = jnp.maximum(c, before[0]) * (wide_b + 1.0) * (wide_b + 2.0)
        w_a = jnp.where(last, 1.0, 0.5)
        w_b = jnp.where(first, 1.0, 0.5)
        for i, value in enumerate((tau_a, tau_b, w_a, w_b, w_a * c, w_b * c)):
            geo[direction, i] = value
        rest = (1.0 - (w_a + w_b)) * c
        for n in range(MODES):
            dia[direction, n] = HALF[n] * (tau_a + tau_b + (2.0 * SLOPE[n]) * rest)

    row, lane = rows((8, 128)), lanes((8, 128))
    prepare(2, (prev_z(c), prev_z(df[2])), (next_z(c), next_z(df[2])), lane == 0, lane == 127)
    for d in range(4):
        @pl.when(source[d])
        def _(d=d):
            param_copy(d).wait_recv()
    px, py = gx * 2 + (row >> 2), gy * 4 + (row & 3)
    prepare(0, prev_x(c, df[0], pg[0]), next_x(c, df[0], pg[1]), px == 0, px == 2 * nx - 1)
    prepare(1, prev_y(c, df[1], pg[2]), next_y(c, df[1], pg[3]), py == 0, py == 4 * ny - 1)

    first_scale, pairs = chebyshev()
    odds = 2.0 * levels.astype(F32) + 1.0

    def setup(a, _):
        for b in range(MODES):
            inside = jnp.where(deg[0] >= a, jnp.where(deg[1] >= b, 1.0, 0.0), 0.0)
            i = (inside[None] * zm[...]) / ((dia[0, a] + dia[1, b])[None] + dia[2])
            r = rhs[a, b] * (odds * ((2.0 * a.astype(F32) + 1.0) * ((2.0 * b + 1.0) / 8.0)))
            x = i * r * first_scale
            s[a, b] = r
            inv[a, b] = i
            step[a, b] = x
            u[a, b] = x
        return 0
    lax.fori_loop(0, MODES, setup, 0)

    def geom(direction):
        return tuple(geo[direction, i][None] for i in range(6))

    def start(make, k, at, base):
        for d in range(2):
            @pl.when(exists[base + d])
            def _(d=d):
                make(k, d, at).start()

    def arrive(make, k, at, base):
        for d in range(2):
            @pl.when(source[base + d])
            def _(d=d):
                make(k, d, at).wait_recv()

    def send_x(k, b, values):
        (tp, tm, fp, fm), _ = line(values, half_coef[None])
        up, down = pack_x_up(tp, fp), pack_x_down(tm, fm)
        if k < 2:
            xs[k, 0, b] = up
            xs[k, 1, b] = down
        else:
            xs3[0, b] = up
            xs3[1, b] = down
        start(x_copy, k, b, 0)

    def first_x(b, _):
        send_x(0, b, [u[n, b] for n in range(MODES)])
        return 0
    lax.fori_loop(0, MODES, first_x, 0)

    for k in range(3):
        count = MODES if k < 2 else CMODES

        def traces_y(a, _):
            (tp, tm, fp, fm), _ = line([u[a, n, 0:count] for n in range(MODES)], half_coef[None])
            up, down = pack_y_up(tp, fp), pack_y_down(tm, fm)
            if k < 2:
                ys[k, 0, a] = up
                ys[k, 1, a] = down
            else:
                ys3[0, a] = up
                ys3[1, a] = down
            start(y_copy, k, a, 2)
            return 0
        lax.fori_loop(0, count, traces_y, 0)

        def pass_z(a, _):
            traces, sums = line([u[a, 0:count, n] for n in range(MODES)], half_coef[None])
            tp, tm, fp, fm = traces
            out = spread(traces, (prev_z(tp), prev_z(fp)), (next_z(tm), next_z(fm)),
                         geom(2), c[None], sums, count)
            for n in range(count):
                acc[a, 0:count, n] = out[n]
            return 0
        lax.fori_loop(0, count, pass_z, 0)

        def pass_y(a, _):
            arrive(y_copy, k, a, 2)
            traces, sums = line([u[a, n, 0:count] for n in range(MODES)], half_coef[None])
            tp, tm, fp, fm = traces
            g_prev = yg[k, 0, a] if k < 2 else yg3[0, a]
            g_next = yg[k, 1, a] if k < 2 else yg3[1, a]
            out = spread(traces, prev_y(tp, fp, g_prev), next_y(tm, fm, g_next),
                         geom(1), c[None], sums, count)
            for n in range(count):
                acc[a, n, 0:count] += out[n]
            return 0
        lax.fori_loop(0, count, pass_y, 0)

        def pass_x(b, _, following=False):
            arrive(x_copy, k, b, 0)
            values = [u[n, b, 0:count] for n in range(MODES)]
            traces, sums = line(values, half_coef[None])
            tp, tm, fp, fm = traces
            g_prev = xg[k, 0, b] if k < 2 else xg3[0, b]
            g_next = xg[k, 1, b] if k < 2 else xg3[1, b]
            out = spread(traces, prev_x(tp, fp, g_prev), next_x(tm, fm, g_next),
                         geom(0), c[None], sums, count)
            if k < 2:
                fresh = []
                for n in range(MODES):
                    residual = s[n, b] - (acc[n, b] + out[n])
                    change = pairs[k][0] * step[n, b] + pairs[k][1] * (inv[n, b] * residual)
                    moved = values[n] + change
                    if k < 1:
                        step[n, b] = change
                    u[n, b] = moved
                    fresh.append(moved)
                if following:
                    width = MODES if k < 1 else CMODES
                    send_x(k + 1, b, [v[0:width] for v in fresh])
            else:
                low = lax.broadcasted_iota(jnp.int32, (CMODES, 8, 128), 0)
                inside_z = jnp.where(low <= (deg[2] >> 1)[None], 1.0, 0.0)
                inside_y = jnp.where((deg[1] >> 1) >= b, 1.0, 0.0)
                mass = (1.0 / ((2.0 * low.astype(F32) + 1.0) * (2.0 * b.astype(F32) + 1.0))) * (
                    inside_z * inside_y[None])
                for n in range(CMODES):
                    inside = jnp.where((deg[0] >> 1) >= n, 8.0 / (2.0 * n + 1.0), 0.0)
                    residual = s[n, b, 0:CMODES] - (acc[n, b, 0:CMODES] + out[n])
                    coarse[n, b] = residual * (mass * inside[None])
            return 0
        if k == 0:
            lax.fori_loop(0, MODES, functools.partial(pass_x, following=True), 0)
        elif k == 1:
            lax.fori_loop(0, CMODES, functools.partial(pass_x, following=True), 0)
            lax.fori_loop(CMODES, MODES, pass_x, 0)
        else:
            lax.fori_loop(0, CMODES, pass_x, 0)

    for d in range(4):
        @pl.when(exists[d])
        def _(d=d):
            param_copy(d).wait_send()
            make = (x_copy, y_copy)[d // 2]
            for k in range(3):
                def finish(i, _):
                    make(k, d % 2, i).wait_send()
                    return 0
                lax.fori_loop(0, MODES if k < 2 else CMODES, finish, 0)


def smoother(nx, ny, rhs, coef, deg):
    field = pltpu.VMEM((MODES, MODES, MODES, 8, 128), F32)
    wide = pltpu.VMEM((2, 2, MODES, MODES, 8, 128), F32)
    narrow = pltpu.VMEM((2, CMODES, CMODES, 8, 128), F32)
    return pl.pallas_call(
        functools.partial(kernel, nx, ny),
        out_shape=(jax.ShapeDtypeStruct((MODES, MODES, MODES, 8, 128), F32),
                   jax.ShapeDtypeStruct((CMODES, CMODES, CMODES, 8, 128), F32)),
        in_specs=[pl.BlockSpec(memory_space=pltpu.VMEM)] * 3,
        out_specs=[pl.BlockSpec(memory_space=pltpu.VMEM)] * 2,
        scratch_shapes=[
            field, field, field, field,
            pltpu.VMEM((3, 6, 8, 128), F32),
            pltpu.VMEM((3, MODES, 8, 128), F32),
            pltpu.VMEM((MODES, 8, 128), F32),
            pltpu.VMEM((4, 8, 128), F32),
            pltpu.VMEM((4, 8, 128), F32),
            wide, wide, wide, wide, narrow, narrow, narrow, narrow,
            pltpu.SemaphoreType.DMA((4,)),
            pltpu.SemaphoreType.DMA((4,)),
            pltpu.SemaphoreType.DMA((3, 2, MODES)),
            pltpu.SemaphoreType.DMA((3, 2, MODES)),
            pltpu.SemaphoreType.DMA((3, 2, MODES)),
            pltpu.SemaphoreType.DMA((3, 2, MODES)),
        ],
        compiler_params=pltpu.CompilerParams(
            collective_id=0, has_side_effects=True, vmem_limit_bytes=48 * 1024 * 1024
        ),
    )(rhs, coef, deg)


def solution(mesh):
    nx, ny = mesh.shape["gx"], mesh.shape["gy"]

    def body(right_side, coefficient, degrees):
        local = right_side.shape[3:]
        flat = (local[0] * local[1], local[2])
        smoothed, coarse = smoother(
            nx, ny,
            right_side.reshape(right_side.shape[:3] + flat),
            coefficient.reshape(flat),
            degrees.reshape((3,) + flat),
        )
        coarse = jnp.transpose(coarse.reshape((CMODES**3,) + local), (0, 1, 3, 2))
        folded = lax.all_to_all(coarse, "gy", split_axis=2, concat_axis=3, tiled=True)
        return (smoothed.reshape(right_side.shape),
                folded.reshape(folded.shape[0], folded.shape[1], -1))

    in_specs = (
        P(None, None, None, "gx", "gy", None),
        P("gx", "gy", None),
        P(None, "gx", "gy", None),
    )
    out_specs = (P(None, None, None, "gx", "gy", None), P(None, "gx", "gy"))
    return jax.shard_map(body, mesh=mesh, in_specs=in_specs, out_specs=out_specs, check_vma=False)
```

profile of v0, /device:TPU:17, one launch (start us, length us, event | category | flops | bytes accessed | tf_op | source)
XLA Modules:
  0.0 48.8 jit_solution(9613589966325238948)
XLA Ops:
  0.6 0.0 copy-start
  0.6 1.3 %copy-done = f32[7,7,7,2,4,128]{5,4,3,2,1,0:T(4,128)S(1)} copy-done((f32[7,7,7,2,4,128]{5,4,3,2,1,0:T(4,128)S(1)}, f32[7,7,7,2,4,128]{5,4,3,2,1,0:T(4,128)}, u32[]{:S(2)}) %copy-start) | copy-done | bytes 1404952
  2.0 0.0 copy-start.1
  2.0 0.7 %copy-done.1 = s32[3,2,4,128]{3,2,1,0:T(4,128)S(1)} copy-done((s32[3,2,4,128]{3,2,1,0:T(4,128)S(1)}, s32[3,2,4,128]{3,2,1,0:T(4,128)}, u32[]{:S(2)}) %copy-start.1) | copy-done | bytes 12312
  2.7 0.0 copy-start.2
  2.7 0.7 %copy-done.2 = f32[2,4,128]{2,1,0:T(4,128)S(1)} copy-done((f32[2,4,128]{2,1,0:T(4,128)S(1)}, f32[2,4,128]{2,1,0:T(4,128)}, u32[]{:S(2)}) %copy-start.2) | copy-done | bytes 4120
  3.4 31.2 %shard_map.50 = (f32[7,7,7,8,128]{4,3,2,1,0:T(8,128)S(1)}, f32[4,4,4,8,128]{4,3,2,1,0:T(8,128)S(1)}) custom-call(f32[7,7,7,8,128]{4,3,2,1,0:T(8,128)S(1)} %bitcast.14, f32[8,128]{1,0:T(8,128)S(1)} %bitcast.18, s32[3,8,128]{2,1,0:T(8,128)S(1)} %bitcast.17), custom_call_target="tpu_custom_call" | custom-call | tf_op jit(solution)/shard_map/pallas_call | solution.py:359
  34.6 0.3 copy.9
  34.9 1.2 %reshape.29 = f32[4,1,16384]{2,1,0:T(1,128)} reshape(f32[128,2,4,64]{3,2,1,0:T(4,128)S(1)} %bitcast_bitcast_fusion) | data formatting | bytes 524288
  36.1 3.4 %all-to-all-start = ((f32[4,1,16384]{2,1,0:T(1,128)}), f32[4,1,16384]{2,1,0:T(1,128)S(1)}, u32[]{:S(2)}, u32[]{:S(2)}) async-start(f32[4,1,16384]{2,1,0:T(1,128)} %reshape.29), calls=%async_computation | async-start | bytes 524288 | tf_op jit(solution)/shard_map/all_to_all | solution.py:399
  39.5 4.6 %all-to-all-done = f32[4,1,16384]{2,1,0:T(1,128)S(1)} async-done(((f32[4,1,16384]{2,1,0:T(1,128)}), f32[4,1,16384]{2,1,0:T(1,128)S(1)}, u32[]{:S(2)}, u32[]{:S(2)}) %all-to-all-start) | async-done | bytes 262176 | tf_op jit(solution)/shard_map/all_to_all | solution.py:399
  44.1 0.5 %broadcast = f32[]{:T(128)} broadcast(f32[]{:T(128)} %constant.3), dimensions={} | broadcast | bytes 8 | tf_op jit(solution)/shard_map/all_to_all | solution.py:399
  44.6 1.4 %reduce = f32[4,16384]{1,0:T(4,128)S(1)} reduce(f32[4,1,16384]{2,1,0:T(1,128)S(1)} %all-to-all-done, f32[]{:T(128)} %broadcast), dimensions={1}, to_apply=%all_to_all.11.reduce_sub_computation | reduce | bytes 524292 | tf_op jit(solution)/shard_map/all_to_all | solution.py:399
  46.0 0.4 reshape.30
  46.4 0.1 copy.10
  46.5 0.3 copy.11
  46.9 0.9 %copy.12 = f32[64,2,512]{2,1,0:T(2,128)} copy(f32[64,2,512]{0,2,1:T(8,128)S(1)} %bitcast.21) | data formatting | bytes 524288
  47.8 1.1 %copy.14 = f32[7,7,7,2,4,128]{5,4,3,2,1,0:T(4,128)} copy(f32[7,7,7,2,4,128]{5,4,3,2,1,0:T(4,128)S(1)} %bitcast.15) | data formatting | bytes 2809856
  (1 shorter events, 0.0 us)
Async XLA Ops:
  0.6 1.4 %copy-start = (f32[7,7,7,2,4,128]{5,4,3,2,1,0:T(4,128)S(1)}, f32[7,7,7,2,4,128]{5,4,3,2,1,0:T(4,128)}, u32[]{:S(2)}) copy-start(f32[7,7,7,2,4,128]{5,4,3,2,1,0:T(4,128)} %param.3) | copy-start | bytes 4214788
  2.0 0.7 %copy-start.1 = (s32[3,2,4,128]{3,2,1,0:T(4,128)S(1)}, s32[3,2,4,128]{3,2,1,0:T(4,128)}, u32[]{:S(2)}) copy-start(s32[3,2,4,128]{3,2,1,0:T(4,128)} %param.5) | copy-start | bytes 36868
  2.7 0.7 %copy-start.2 = (f32[2,4,128]{2,1,0:T(4,128)S(1)}, f32[2,4,128]{2,1,0:T(4,128)}, u32[]{:S(2)}) copy-start(f32[2,4,128]{2,1,0:T(4,128)} %param.4) | copy-start | bytes 12292
  36.1 8.0 %all-to-all-start = ((f32[4,1,16384]{2,1,0:T(1,128)}), f32[4,1,16384]{2,1,0:T(1,128)S(1)}, u32[]{:S(2)}, u32[]{:S(2)}) async-start(f32[4,1,16384]{2,1,0:T(1,128)} %reshape.29), calls=%async_computation | async-start | bytes 524288 | tf_op jit(solution)/shard_map/all_to_all | solution.py:399
where the time goes:
time: 49.5 us; the launch traced here: 48.8 us
  Pallas kernels  31.2 us (63%)
  local copies, waits for them, and re-layouts  7.56 us (15%)
  waiting for transfers between devices  4.64 us (9%)
  starting transfers between devices  3.4 us (7%)
  other arithmetic  1.38 us (3%)
  between operations  0.69 us (1%)
    pallas_call x1, Pallas kernels, smoother(): pl.pallas_call(functools.partial(kernel, nx, ny), out_shape=(jax.ShapeDty...  31.2 us
    unnamed x11, local copies, waits for them, and re-layouts  6.32 us
    all_to_all x1, waiting for transfers between devices, body(): lax.all_to_all(coarse, 'gy', split_axis=2, concat_axis=3, tiled=True)  4.64 us
    all_to_all x1, starting transfers between devices, body(): lax.all_to_all(coarse, 'gy', split_axis=2, concat_axis=3, tiled=True)  3.4 us
    all_to_all x1, other arithmetic, body(): lax.all_to_all(coarse, 'gy', split_axis=2, concat_axis=3, tiled=True)  1.38 us
  transfers between devices with their start and end apart: 1, of which 1 were waited for; matrix products, arithmetic and copies ran while one was open for 0% of the time, Pallas kernels for 0%

commit v1 on v0

--- a/solution.py
+++ b/solution.py
@@ -123,19 +123,27 @@
     return out
 
 
-def kernel(nx, ny, rhs, coef, deg, u, coarse, s, inv, step, acc, geo, dia, zm,
-           ps, pg, xs, xg, ys, yg, xs3, xg3, ys3, yg3,
-           p_send, p_recv, x_send, x_recv, y_send, y_recv):
+def kernel(nx, ny, rhs_hbm, coef_hbm, deg_hbm, u, coarse, s, coef, deg, inv, step, acc, geo, dia, zm,
+           ps, pg, xs, xg, ys, yg, xs3, xg3, ys3, yg3, kept, folds, folded, order,
+           in_sem, p_send, p_recv, x_send, x_recv, y_send, y_recv, f_send, f_recv):
+    loads = [pltpu.make_async_copy(a, b, in_sem.at[i])
+             for i, (a, b) in enumerate(((coef_hbm, coef), (deg_hbm, deg), (rhs_hbm, s)))]
+    for load in loads:
+        load.start()
     gx, gy = lax.axis_index("gx"), lax.axis_index("gy")
     exists = (gx < nx - 1, gx > 0, gy < ny - 1, gy > 0)
     target = ({"gx": gx + 1}, {"gx": gx - 1}, {"gy": gy + 1}, {"gy": gy - 1})
     source = (exists[1], exists[0], exists[3], exists[2])
 
     barrier = pltpu.get_barrier_semaphore()
-    for d in range(4):
+    for d in range(2):
         @pl.when(exists[d])
         def _(d=d):
             pl.semaphore_signal(barrier, inc=1, device_id=target[d], device_id_type=MESH)
+    for d in range(ny):
+        @pl.when(gy != d)
+        def _(d=d):
+            pl.semaphore_signal(barrier, inc=1, device_id={"gy": d}, device_id_type=MESH)
 
     def copy(src, dst, send, recv, d):
         return pltpu.make_async_remote_copy(src_ref=src, dst_ref=dst, send_sem=send, recv_sem=recv,
@@ -154,6 +162,8 @@
             return copy(ys.at[k, d, a], yg.at[k, d, a], y_send.at[k, d, a], y_recv.at[k, d, a], 2 + d)
         return copy(ys3.at[d, a], yg3.at[d, a], y_send.at[k, d, a], y_recv.at[k, d, a], 2 + d)
 
+    loads[0].wait()
+    loads[1].wait()
     c = coef[...]
     half_coef = 0.5 * c
     df = [deg[d].astype(F32) for d in range(3)]
@@ -161,7 +171,7 @@
     ps[1] = pack_x_down(c, df[0])
     ps[2] = pack_y_up(c, df[1])
     ps[3] = pack_y_down(c, df[1])
-    pl.semaphore_wait(barrier, sum(e.astype(jnp.int32) for e in exists))
+    pl.semaphore_wait(barrier, sum(e.astype(jnp.int32) for e in exists[:2]) + (ny - 1))
     for d in range(4):
         @pl.when(exists[d])
         def _(d=d):
@@ -216,19 +226,6 @@
     first_scale, pairs = chebyshev()
     odds = 2.0 * levels.astype(F32) + 1.0
 
-    def setup(a, _):
-        for b in range(MODES):
-            inside = jnp.where(deg[0] >= a, jnp.where(deg[1] >= b, 1.0, 0.0), 0.0)
-            i = (inside[None] * zm[...]) / ((dia[0, a] + dia[1, b])[None] + dia[2])
-            r = rhs[a, b] * (odds * ((2.0 * a.astype(F32) + 1.0) * ((2.0 * b + 1.0) / 8.0)))
-            x = i * r * first_scale
-            s[a, b] = r
-            inv[a, b] = i
-            step[a, b] = x
-            u[a, b] = x
-        return 0
-    lax.fori_loop(0, MODES, setup, 0)
-
     def geom(direction):
         return tuple(geo[direction, i][None] for i in range(6))
 
@@ -255,10 +252,32 @@
             xs3[1, b] = down
         start(x_copy, k, b, 0)
 
-    def first_x(b, _):
-        send_x(0, b, [u[n, b] for n in range(MODES)])
+    loads[2].wait()
+
+    def setup(b, _):
+        inside_y = jnp.where(deg[1] >= b, 1.0, 0.0)[None] * zm[...]
+        across = dia[1, b][None] + dia[2]
+        scale = odds * ((2.0 * b.astype(F32) + 1.0) / 8.0)
+        fresh = []
+        for a in range(MODES):
+            i = jnp.where(deg[0] >= a, 1.0, 0.0)[None] * inside_y / (dia[0, a][None] + across)
+            r = s[a, b] * (scale * (2.0 * a + 1.0))
+            x = i * r * first_scale
+            s[a, b] = r
+            inv[a, b] = i
+            step[a, b] = x
+            u[a, b] = x
+            fresh.append(x)
+        send_x(0, b, fresh)
         return 0
-    lax.fori_loop(0, MODES, first_x, 0)
+    lax.fori_loop(0, MODES, setup, 0)
+
+    source_lane = lax.broadcasted_iota(jnp.int32, (128, 512), 0)
+    fine_lane = lax.broadcasted_iota(jnp.int32, (128, 512), 1)
+    depth = 128 // ny
+    spot = (source_lane % depth) * (4 * ny) + source_lane // depth
+    for d in range(ny):
+        order[d] = jnp.where((source_lane < 4 * depth) & (fine_lane == spot + 4 * d), 1.0, 0.0).astype(jnp.bfloat16)
 
     for k in range(3):
         count = MODES if k < 2 else CMODES
@@ -330,7 +349,7 @@
                 for n in range(CMODES):
                     inside = jnp.where((deg[0] >> 1) >= n, 8.0 / (2.0 * n + 1.0), 0.0)
                     residual = s[n, b, 0:CMODES] - (acc[n, b, 0:CMODES] + out[n])
-                    coarse[n, b] = residual * (mass * inside[None])
+                    kept[n, b] = residual * (mass * inside[None])
             return 0
         if k == 0:
             lax.fori_loop(0, MODES, functools.partial(pass_x, following=True), 0)
@@ -340,6 +359,55 @@
         else:
             lax.fori_loop(0, CMODES, pass_x, 0)
 
+    def fold_copy(d):
+        return pltpu.make_async_remote_copy(
+            src_ref=folds.at[d], dst_ref=folded.at[gy], send_sem=f_send.at[d], recv_sem=f_recv.at[gy],
+            device_id={"gy": d}, device_id_type=MESH)
+
+    def fold_arrival(d):
+        return pltpu.make_async_remote_copy(
+            src_ref=folds.at[d], dst_ref=folded.at[d], send_sem=f_send.at[d], recv_sem=f_recv.at[d],
+            device_id={"gy": d}, device_id_type=MESH)
+
+    cells = kept.reshape(CMODES**3 * 8, 128)
+    block = lanes((CMODES**3, 128)) // depth
+    for x in range(2):
+        by_y = [cells[pl.ds(x * 4 + y, CMODES**3, stride=8), :] for y in range(4)]
+        for d in range(ny):
+            out = jnp.zeros((CMODES**3, 128), F32)
+            for y in range(4):
+                shift = ((y - d) * depth) % 128
+                out = jnp.where(block == y, pltpu.roll(by_y[y], shift, 1) if shift else by_y[y], out)
+            folds[d, x] = out
+    for d in range(ny):
+        @pl.when(gy != d)
+        def _(d=d):
+            fold_copy(d).start()
+
+        @pl.when(gy == d)
+        def _(d=d):
+            folded[d] = folds[d]
+    for d in range(ny):
+        @pl.when(gy != d)
+        def _(d=d):
+            fold_arrival(d).wait_recv()
+    total = jnp.zeros((2 * CMODES**3, 512), F32)
+    for d in range(ny):
+        left = folded[d].reshape(2 * CMODES**3, 128)
+        for part in range(3):
+            piece = left.astype(jnp.bfloat16)
+            total = total + jnp.dot(piece, order[d], preferred_element_type=F32)
+            if part < 2:
+                left = left - piece.astype(F32)
+    for x in range(2):
+        for j in range(4):
+            coarse[pl.ds(j * 2 + x, CMODES**3, stride=8), :] = total[
+                x * CMODES**3:(x + 1) * CMODES**3, j * 128:(j + 1) * 128]
+    for d in range(ny):
+        @pl.when(gy != d)
+        def _(d=d):
+            fold_copy(d).wait_send()
+
     for d in range(4):
         @pl.when(exists[d])
         def _(d=d):
@@ -359,23 +427,33 @@
     return pl.pallas_call(
         functools.partial(kernel, nx, ny),
         out_shape=(jax.ShapeDtypeStruct((MODES, MODES, MODES, 8, 128), F32),
-                   jax.ShapeDtypeStruct((CMODES, CMODES, CMODES, 8, 128), F32)),
-        in_specs=[pl.BlockSpec(memory_space=pltpu.VMEM)] * 3,
+                   jax.ShapeDtypeStruct((CMODES**3 * 8, 128), F32)),
+        in_specs=[pl.BlockSpec(memory_space=pltpu.HBM)] * 3,
         out_specs=[pl.BlockSpec(memory_space=pltpu.VMEM)] * 2,
         scratch_shapes=[
-            field, field, field, field,
+            field,
+            pltpu.VMEM((8, 128), F32),
+            pltpu.VMEM((3, 8, 128), jnp.int32),
+            field, field, field,
             pltpu.VMEM((3, 6, 8, 128), F32),
             pltpu.VMEM((3, MODES, 8, 128), F32),
             pltpu.VMEM((MODES, 8, 128), F32),
             pltpu.VMEM((4, 8, 128), F32),
             pltpu.VMEM((4, 8, 128), F32),
             wide, wide, wide, wide, narrow, narrow, narrow, narrow,
+            pltpu.VMEM((CMODES, CMODES, CMODES, 8, 128), F32),
+            pltpu.VMEM((ny, 2, CMODES**3, 128), F32),
+            pltpu.VMEM((ny, 2, CMODES**3, 128), F32),
+            pltpu.VMEM((ny, 128, 512), jnp.bfloat16),
+            pltpu.SemaphoreType.DMA((3,)),
             pltpu.SemaphoreType.DMA((4,)),
             pltpu.SemaphoreType.DMA((4,)),
             pltpu.SemaphoreType.DMA((3, 2, MODES)),
             pltpu.SemaphoreType.DMA((3, 2, MODES)),
             pltpu.SemaphoreType.DMA((3, 2, MODES)),
             pltpu.SemaphoreType.DMA((3, 2, MODES)),
+            pltpu.SemaphoreType.DMA((ny,)),
+            pltpu.SemaphoreType.DMA((ny,)),
         ],
         compiler_params=pltpu.CompilerParams(
             collective_id=0, has_side_effects=True, vmem_limit_bytes=48 * 1024 * 1024
@@ -395,10 +473,8 @@
             coefficient.reshape(flat),
             degrees.reshape((3,) + flat),
         )
-        coarse = jnp.transpose(coarse.reshape((CMODES**3,) + local), (0, 1, 3, 2))
-        folded = lax.all_to_all(coarse, "gy", split_axis=2, concat_axis=3, tiled=True)
-        return (smoothed.reshape(right_side.shape),
-                folded.reshape(folded.shape[0], folded.shape[1], -1))
+        coarse = jnp.transpose(coarse.reshape(CMODES**3, 4, 2, 128), (0, 2, 1, 3))
+        return smoothed.reshape(right_side.shape), coarse.reshape(CMODES**3, 2, 512)
 
     in_specs = (
         P(None, None, None, "gx", "gy", None),

time: 49.5 us -> 41.4 us (0.84)
  Pallas kernels: 31.2 us -> 35.9 us
  waiting for transfers between devices: 4.64 us -> 0 us
  starting transfers between devices: 3.4 us -> 0 us
  local copies, waits for them, and re-layouts: 7.56 us -> 4.53 us
  other arithmetic: 1.38 us -> 0 us
    pallas_call x1, Pallas kernels: 31.2 us -> 35.9 us  [smoother(): pl.pallas_call(functools.partial(kernel, nx, ny), out_shape=(jax.ShapeDty...]
    all_to_all x1 -> x0, waiting for transfers between devices: 4.64 us -> none  [body(): lax.all_to_all(coarse, 'gy', split_axis=2, concat_axis=3, tiled=True)]
    all_to_all x1 -> x0, starting transfers between devices: 3.4 us -> none  [body(): lax.all_to_all(coarse, 'gy', split_axis=2, concat_axis=3, tiled=True)]
    unnamed x11 -> x8, local copies, waits for them, and re-layouts: 6.32 us -> 4.53 us
    all_to_all x1 -> x0, other arithmetic: 1.38 us -> none  [body(): lax.all_to_all(coarse, 'gy', split_axis=2, concat_axis=3, tiled=True)]
    all_to_all x3 -> x0, local copies, waits for them, and re-layouts: 0.96 us -> none  [body(): lax.all_to_all(coarse, 'gy', split_axis=2, concat_axis=3, tiled=True)]
  transfers between devices with their start and end apart: 1 -> 0, of which waited for: 1 -> 0; matrix products, arithmetic and copies ran while one was open for 0% -> 0% of each run, Pallas kernels for 0% -> 0%
where the time goes in v1:
time: 41.4 us; the launch traced here: 41.1 us
  Pallas kernels  35.9 us (87%)
  local copies, waits for them, and re-layouts  4.53 us (11%)
  between operations  0.65 us (2%)
    pallas_call x1, Pallas kernels, smoother(): pl.pallas_call(functools.partial(kernel, nx, ny), out_shape=(jax.ShapeDty...  35.9 us
    unnamed x8, local copies, waits for them, and re-layouts  4.53 us

profile of v1, /device:TPU:17, one launch (start us, length us, event | category | flops | bytes accessed | tf_op | source)
XLA Modules:
  0.0 41.1 jit_solution(12809212709708188586)
XLA Ops:
  0.6 0.0 copy-start
  0.6 1.3 %copy-done = f32[7,7,7,2,4,128]{5,4,3,2,1,0:T(4,128)S(1)} copy-done((f32[7,7,7,2,4,128]{5,4,3,2,1,0:T(4,128)S(1)}, f32[7,7,7,2,4,128]{5,4,3,2,1,0:T(4,128)}, u32[]{:S(2)}) %copy-start) | copy-done | bytes 1404952
  2.0 0.0 copy-start.1
  2.0 0.7 %copy-done.1 = s32[3,2,4,128]{3,2,1,0:T(4,128)S(1)} copy-done((s32[3,2,4,128]{3,2,1,0:T(4,128)S(1)}, s32[3,2,4,128]{3,2,1,0:T(4,128)}, u32[]{:S(2)}) %copy-start.1) | copy-done | bytes 12312
  2.7 0.0 copy-start.2
  2.7 0.7 %copy-done.2 = f32[2,4,128]{2,1,0:T(4,128)S(1)} copy-done((f32[2,4,128]{2,1,0:T(4,128)S(1)}, f32[2,4,128]{2,1,0:T(4,128)}, u32[]{:S(2)}) %copy-start.2) | copy-done | bytes 4120
  3.4 35.9 %shard_map.50 = (f32[7,7,7,8,128]{4,3,2,1,0:T(8,128)S(1)}, f32[512,128]{1,0:T(8,128)S(1)}) custom-call(f32[7,7,7,8,128]{4,3,2,1,0:T(8,128)S(1)} %bitcast.9, f32[8,128]{1,0:T(8,128)S(1)} %bitcast.13, s32[3,8,128]{2,1,0:T(8,128)S(1)} %bitcast.12), custom_call_target="tpu_custom_call" | custom-call | tf_op jit(solution)/shard_map/pallas_call | solution.py:427
  39.3 1.1 %copy.8 = f32[7,7,7,2,4,128]{5,4,3,2,1,0:T(4,128)} copy(f32[7,7,7,2,4,128]{5,4,3,2,1,0:T(4,128)S(1)} %bitcast.10) | data formatting | bytes 2809856
  40.4 0.7 %copy.9 = f32[64,2,512]{2,1,0:T(2,128)} copy(f32[64,2,512]{2,1,0:T(2,128)S(1)} %bitcast.11) | data formatting | bytes 524288
Async XLA Ops:
  0.6 1.4 %copy-start = (f32[7,7,7,2,4,128]{5,4,3,2,1,0:T(4,128)S(1)}, f32[7,7,7,2,4,128]{5,4,3,2,1,0:T(4,128)}, u32[]{:S(2)}) copy-start(f32[7,7,7,2,4,128]{5,4,3,2,1,0:T(4,128)} %param.3) | copy-start | bytes 4214788
  2.0 0.7 %copy-start.1 = (s32[3,2,4,128]{3,2,1,0:T(4,128)S(1)}, s32[3,2,4,128]{3,2,1,0:T(4,128)}, u32[]{:S(2)}) copy-start(s32[3,2,4,128]{3,2,1,0:T(4,128)} %param.5) | copy-start | bytes 36868
  2.7 0.7 %copy-start.2 = (f32[2,4,128]{2,1,0:T(4,128)S(1)}, f32[2,4,128]{2,1,0:T(4,128)}, u32[]{:S(2)}) copy-start(f32[2,4,128]{2,1,0:T(4,128)} %param.4) | copy-start | bytes 12292

commit v2 on v1

--- a/solution.py
+++ b/solution.py
@@ -166,6 +166,7 @@
     loads[1].wait()
     c = coef[...]
     half_coef = 0.5 * c
+    depth = 128 // ny
     df = [deg[d].astype(F32) for d in range(3)]
     ps[0] = pack_x_up(c, df[0])
     ps[1] = pack_x_down(c, df[0])
@@ -176,6 +177,12 @@
         @pl.when(exists[d])
         def _(d=d):
             param_copy(d).start()
+
+    source_lane = lax.broadcasted_iota(jnp.int32, (128, 512), 0)
+    fine_lane = lax.broadcasted_iota(jnp.int32, (128, 512), 1)
+    spot = (source_lane % depth) * (4 * ny) + source_lane // depth
+    for d in range(ny):
+        order[d * 128:(d + 1) * 128] = jnp.where((source_lane < 4 * depth) & (fine_lane == spot + 4 * d), 1.0, 0.0).astype(jnp.bfloat16)
 
     for d in range(4):
         @pl.when(jnp.logical_not(source[d]))
@@ -272,12 +279,34 @@
         return 0
     lax.fori_loop(0, MODES, setup, 0)
 
-    source_lane = lax.broadcasted_iota(jnp.int32, (128, 512), 0)
-    fine_lane = lax.broadcasted_iota(jnp.int32, (128, 512), 1)
-    depth = 128 // ny
-    spot = (source_lane % depth) * (4 * ny) + source_lane // depth
-    for d in range(ny):
-        order[d] = jnp.where((source_lane < 4 * depth) & (fine_lane == spot + 4 * d), 1.0, 0.0).astype(jnp.bfloat16)
+    def fold_copy(d, b):
+        return pltpu.make_async_remote_copy(
+            src_ref=folds.at[d, b], dst_ref=folded.at[gy, b], send_sem=f_send.at[d, b],
+            recv_sem=f_recv.at[gy, b], device_id={"gy": d}, device_id_type=MESH)
+
+    def fold_arrival(d, b):
+        return pltpu.make_async_remote_copy(
+            src_ref=folds.at[d, b], dst_ref=folded.at[d, b], send_sem=f_send.at[d, b],
+            recv_sem=f_recv.at[d, b], device_id={"gy": d}, device_id_type=MESH)
+
+    def fold(b):
+        block = lanes((CMODES**2, 128)) // depth
+        for x in range(2):
+            by_y = [kept[b, pl.ds(x * 4 + y, CMODES**2, stride=8), :] for y in range(4)]
+            for d in range(ny):
+                out = jnp.zeros((CMODES**2, 128), F32)
+                for y in range(4):
+                    shift = ((y - d) * depth) % 128
+                    out = jnp.where(block == y, pltpu.roll(by_y[y], shift, 1) if shift else by_y[y], out)
+                folds[d, b, x] = out
+        for d in range(ny):
+            @pl.when(gy != d)
+            def _(d=d):
+                fold_copy(d, b).start()
+
+            @pl.when(gy == d)
+            def _(d=d):
+                folded[d, b] = folds[d, b]
 
     for k in range(3):
         count = MODES if k < 2 else CMODES
@@ -349,7 +378,8 @@
                 for n in range(CMODES):
                     inside = jnp.where((deg[0] >> 1) >= n, 8.0 / (2.0 * n + 1.0), 0.0)
                     residual = s[n, b, 0:CMODES] - (acc[n, b, 0:CMODES] + out[n])
-                    kept[n, b] = residual * (mass * inside[None])
+                    kept[b, n * 32:(n + 1) * 32] = (residual * (mass * inside[None])).reshape(32, 128)
+                fold(b)
             return 0
         if k == 0:
             lax.fori_loop(0, MODES, functools.partial(pass_x, following=True), 0)
@@ -359,54 +389,29 @@
         else:
             lax.fori_loop(0, CMODES, pass_x, 0)
 
-    def fold_copy(d):
-        return pltpu.make_async_remote_copy(
-            src_ref=folds.at[d], dst_ref=folded.at[gy], send_sem=f_send.at[d], recv_sem=f_recv.at[gy],
-            device_id={"gy": d}, device_id_type=MESH)
-
-    def fold_arrival(d):
-        return pltpu.make_async_remote_copy(
-            src_ref=folds.at[d], dst_ref=folded.at[d], send_sem=f_send.at[d], recv_sem=f_recv.at[d],
-            device_id={"gy": d}, device_id_type=MESH)
-
-    cells = kept.reshape(CMODES**3 * 8, 128)
-    block = lanes((CMODES**3, 128)) // depth
-    for x in range(2):
-        by_y = [cells[pl.ds(x * 4 + y, CMODES**3, stride=8), :] for y in range(4)]
-        for d in range(ny):
-            out = jnp.zeros((CMODES**3, 128), F32)
-            for y in range(4):
-                shift = ((y - d) * depth) % 128
-                out = jnp.where(block == y, pltpu.roll(by_y[y], shift, 1) if shift else by_y[y], out)
-            folds[d, x] = out
     for d in range(ny):
         @pl.when(gy != d)
         def _(d=d):
-            fold_copy(d).start()
-
-        @pl.when(gy == d)
-        def _(d=d):
-            folded[d] = folds[d]
+            for b in range(CMODES):
+                fold_arrival(d, b).wait_recv()
+    left = jnp.concatenate([folded[d].reshape(2 * CMODES**3, 128) for d in range(ny)], axis=1)
+    total = jnp.zeros((2 * CMODES**3, 512), F32)
+    for part in range(3):
+        piece = left.astype(jnp.bfloat16)
+        total = total + jnp.dot(piece, order[...], preferred_element_type=F32)
+        if part < 2:
+            left = left - piece.astype(F32)
+    for b in range(CMODES):
+        for x in range(2):
+            for n in range(CMODES):
+                for j in range(4):
+                    coarse[pl.ds((n * 16 + b * 4) * 8 + j * 2 + x, CMODES, stride=8), :] = total[
+                        b * 32 + x * 16 + n * 4:b * 32 + x * 16 + n * 4 + 4, j * 128:(j + 1) * 128]
     for d in range(ny):
         @pl.when(gy != d)
         def _(d=d):
-            fold_arrival(d).wait_recv()
-    total = jnp.zeros((2 * CMODES**3, 512), F32)
-    for d in range(ny):
-        left = folded[d].reshape(2 * CMODES**3, 128)
-        for part in range(3):
-            piece = left.astype(jnp.bfloat16)
-            total = total + jnp.dot(piece, order[d], preferred_element_type=F32)
-            if part < 2:
-                left = left - piece.astype(F32)
-    for x in range(2):
-        for j in range(4):
-            coarse[pl.ds(j * 2 + x, CMODES**3, stride=8), :] = total[
-                x * CMODES**3:(x + 1) * CMODES**3, j * 128:(j + 1) * 128]
-    for d in range(ny):
-        @pl.when(gy != d)
-        def _(d=d):
-            fold_copy(d).wait_send()
+            for b in range(CMODES):
+                fold_copy(d, b).wait_send()
 
     for d in range(4):
         @pl.when(exists[d])
@@ -441,10 +446,10 @@
             pltpu.VMEM((4, 8, 128), F32),
             pltpu.VMEM((4, 8, 128), F32),
             wide, wide, wide, wide, narrow, narrow, narrow, narrow,
-            pltpu.VMEM((CMODES, CMODES, CMODES, 8, 128), F32),
-            pltpu.VMEM((ny, 2, CMODES**3, 128), F32),
-            pltpu.VMEM((ny, 2, CMODES**3, 128), F32),
-            pltpu.VMEM((ny, 128, 512), jnp.bfloat16),
+            pltpu.VMEM((CMODES, 128, 128), F32),
+            pltpu.VMEM((ny, CMODES, 2, CMODES**2, 128), F32),
+            pltpu.VMEM((ny, CMODES, 2, CMODES**2, 128), F32),
+            pltpu.VMEM((ny * 128, 512), jnp.bfloat16),
             pltpu.SemaphoreType.DMA((3,)),
             pltpu.SemaphoreType.DMA((4,)),
             pltpu.SemaphoreType.DMA((4,)),
@@ -452,13 +457,13 @@
             pltpu.SemaphoreType.DMA((3, 2, MODES)),
             pltpu.SemaphoreType.DMA((3, 2, MODES)),
             pltpu.SemaphoreType.DMA((3, 2, MODES)),
-            pltpu.SemaphoreType.DMA((ny,)),
-            pltpu.SemaphoreType.DMA((ny,)),
+            pltpu.SemaphoreType.DMA((ny, CMODES)),
+            pltpu.SemaphoreType.DMA((ny, CMODES)),
         ],
         compiler_params=pltpu.CompilerParams(
             collective_id=0, has_side_effects=True, vmem_limit_bytes=48 * 1024 * 1024
         ),
-    )(rhs, coef, deg)
+    )(*(pltpu.with_memory_space_constraint(v, pltpu.HBM) for v in (rhs, coef, deg)))
 
 
 def solution(mesh):

time: 41.4 us -> 38.2 us (0.923)
  local copies, waits for them, and re-layouts: 4.53 us -> 1.79 us
    unnamed x8 -> x2, local copies, waits for them, and re-layouts: 4.53 us -> 1.79 us
where the time goes in v2:
time: 38.2 us; the launch traced here: 38 us
  Pallas kernels  35.6 us (93%)
  local copies, waits for them, and re-layouts  1.79 us (5%)
  between operations  0.64 us (2%)
    pallas_call x1, Pallas kernels, smoother(): pl.pallas_call(functools.partial(kernel, nx, ny), out_shape=(jax.ShapeDty...  35.6 us
    unnamed x2, local copies, waits for them, and re-layouts  1.79 us

profile of v2, /device:TPU:17, one launch (start us, length us, event | category | flops | bytes accessed | tf_op | source)
XLA Modules:
  0.0 38.0 jit_solution(14573522212431803438)
XLA Ops:
  0.6 35.6 %shard_map.50 = (f32[7,7,7,8,128]{4,3,2,1,0:T(8,128)S(1)}, f32[512,128]{1,0:T(8,128)S(1)}) custom-call(f32[7,7,7,8,128]{4,3,2,1,0:T(8,128)} %bitcast.11, f32[8,128]{1,0:T(8,128)} %bitcast.13, s32[3,8,128]{2,1,0:T(8,128)} %bitcast.12), custom_call_target="tpu_custom_call" | custom-call | tf_op jit(solution)/shard_map/pallas_call | solution.py:432
  36.2 1.1 %copy.8 = f32[7,7,7,2,4,128]{5,4,3,2,1,0:T(4,128)} copy(f32[7,7,7,2,4,128]{5,4,3,2,1,0:T(4,128)S(1)} %bitcast.9) | data formatting | bytes 2809856
  37.3 0.7 %copy.9 = f32[64,2,512]{2,1,0:T(2,128)} copy(f32[64,2,512]{2,1,0:T(2,128)S(1)} %bitcast.10) | data formatting | bytes 524288

commit v3 on v2

--- a/solution.py
+++ b/solution.py
@@ -123,8 +123,8 @@
     return out
 
 
-def kernel(nx, ny, rhs_hbm, coef_hbm, deg_hbm, u, coarse, s, coef, deg, inv, step, acc, geo, dia, zm,
-           ps, pg, xs, xg, ys, yg, xs3, xg3, ys3, yg3, kept, folds, folded, order,
+def kernel(nx, ny, rhs_hbm, coef_hbm, deg_hbm, u, left, s, coef, deg, inv, step, acc, geo, dia, zm,
+           ps, pg, xs, xg, ys, yg, xs3, xg3, ys3, yg3, kept, folds, folded,
            in_sem, p_send, p_recv, x_send, x_recv, y_send, y_recv, f_send, f_recv):
     loads = [pltpu.make_async_copy(a, b, in_sem.at[i])
              for i, (a, b) in enumerate(((coef_hbm, coef), (deg_hbm, deg), (rhs_hbm, s)))]
@@ -177,12 +177,6 @@
         @pl.when(exists[d])
         def _(d=d):
             param_copy(d).start()
-
-    source_lane = lax.broadcasted_iota(jnp.int32, (128, 512), 0)
-    fine_lane = lax.broadcasted_iota(jnp.int32, (128, 512), 1)
-    spot = (source_lane % depth) * (4 * ny) + source_lane // depth
-    for d in range(ny):
-        order[d * 128:(d + 1) * 128] = jnp.where((source_lane < 4 * depth) & (fine_lane == spot + 4 * d), 1.0, 0.0).astype(jnp.bfloat16)
 
     for d in range(4):
         @pl.when(jnp.logical_not(source[d]))
@@ -300,7 +294,11 @@
                     out = jnp.where(block == y, pltpu.roll(by_y[y], shift, 1) if shift else by_y[y], out)
                 folds[d, b, x] = out
         for d in range(ny):
-            @pl.when(gy != d)
+            @pl.when(gy // 2 != d // 2)
+            def _(d=d):
+                fold_copy(d, b).start()
+        for d in range(ny):
+            @pl.when((gy // 2 == d // 2) & (gy != d))
             def _(d=d):
                 fold_copy(d, b).start()
 
@@ -394,19 +392,8 @@
         def _(d=d):
             for b in range(CMODES):
                 fold_arrival(d, b).wait_recv()
-    left = jnp.concatenate([folded[d].reshape(2 * CMODES**3, 128) for d in range(ny)], axis=1)
-    total = jnp.zeros((2 * CMODES**3, 512), F32)
-    for part in range(3):
-        piece = left.astype(jnp.bfloat16)
-        total = total + jnp.dot(piece, order[...], preferred_element_type=F32)
-        if part < 2:
-            left = left - piece.astype(F32)
-    for b in range(CMODES):
-        for x in range(2):
-            for n in range(CMODES):
-                for j in range(4):
-                    coarse[pl.ds((n * 16 + b * 4) * 8 + j * 2 + x, CMODES, stride=8), :] = total[
-                        b * 32 + x * 16 + n * 4:b * 32 + x * 16 + n * 4 + 4, j * 128:(j + 1) * 128]
+    for d in range(ny):
+        left[:, d * 128:(d + 1) * 128] = folded[d].reshape(2 * CMODES**3, 128)
     for d in range(ny):
         @pl.when(gy != d)
         def _(d=d):
@@ -432,7 +419,7 @@
     return pl.pallas_call(
         functools.partial(kernel, nx, ny),
         out_shape=(jax.ShapeDtypeStruct((MODES, MODES, MODES, 8, 128), F32),
-                   jax.ShapeDtypeStruct((CMODES**3 * 8, 128), F32)),
+                   jax.ShapeDtypeStruct((2 * CMODES**3, ny * 128), F32)),
         in_specs=[pl.BlockSpec(memory_space=pltpu.HBM)] * 3,
         out_specs=[pl.BlockSpec(memory_space=pltpu.VMEM)] * 2,
         scratch_shapes=[
@@ -449,7 +436,6 @@
             pltpu.VMEM((CMODES, 128, 128), F32),
             pltpu.VMEM((ny, CMODES, 2, CMODES**2, 128), F32),
             pltpu.VMEM((ny, CMODES, 2, CMODES**2, 128), F32),
-            pltpu.VMEM((ny * 128, 512), jnp.bfloat16),
             pltpu.SemaphoreType.DMA((3,)),
             pltpu.SemaphoreType.DMA((4,)),
             pltpu.SemaphoreType.DMA((4,)),
@@ -466,18 +452,56 @@
     )(*(pltpu.with_memory_space_constraint(v, pltpu.HBM) for v in (rhs, coef, deg)))
 
 
+def finish_kernel(ny, u, blocks, stored, coarse, order, sem):
+    copy = pltpu.make_async_copy(u, stored, sem)
+    copy.start()
+    depth = 128 // ny
+    source_lane = lax.broadcasted_iota(jnp.int32, (128, 512), 0)
+    fine_lane = lax.broadcasted_iota(jnp.int32, (128, 512), 1)
+    spot = (source_lane % depth) * (4 * ny) + source_lane // depth
+    for d in range(ny):
+        order[d * 128:(d + 1) * 128] = jnp.where((source_lane < 4 * depth) & (fine_lane == spot + 4 * d), 1.0, 0.0).astype(jnp.bfloat16)
+    left = blocks[...]
+    total = jnp.zeros((2 * CMODES**3, 512), F32)
+    for part in range(3):
+        piece = left.astype(jnp.bfloat16)
+        total = total + jnp.dot(piece, order[...], preferred_element_type=F32)
+        if part < 2:
+            left = left - piece.astype(F32)
+    for b in range(CMODES):
+        for x in range(2):
+            for n in range(CMODES):
+                for j in range(4):
+                    coarse[pl.ds((n * 16 + b * 4) * 8 + j * 2 + x, CMODES, stride=8), :] = total[
+                        b * 32 + x * 16 + n * 4:b * 32 + x * 16 + n * 4 + 4, j * 128:(j + 1) * 128]
+    copy.wait()
+
+
+def finish(ny, u, blocks):
+    return pl.pallas_call(
+        functools.partial(finish_kernel, ny),
+        out_shape=(jax.ShapeDtypeStruct(u.shape, F32),
+                   jax.ShapeDtypeStruct((CMODES**3 * 8, 128), F32)),
+        in_specs=[pl.BlockSpec(memory_space=pl.ANY), pl.BlockSpec(memory_space=pltpu.VMEM)],
+        out_specs=[pl.BlockSpec(memory_space=pltpu.HBM), pl.BlockSpec(memory_space=pltpu.VMEM)],
+        scratch_shapes=[pltpu.VMEM((ny * 128, 512), jnp.bfloat16), pltpu.SemaphoreType.DMA],
+        compiler_params=pltpu.CompilerParams(vmem_limit_bytes=16 * 1024 * 1024),
+    )(u, blocks)
+
+
 def solution(mesh):
     nx, ny = mesh.shape["gx"], mesh.shape["gy"]
 
     def body(right_side, coefficient, degrees):
         local = right_side.shape[3:]
         flat = (local[0] * local[1], local[2])
-        smoothed, coarse = smoother(
+        smoothed, blocks = smoother(
             nx, ny,
             right_side.reshape(right_side.shape[:3] + flat),
             coefficient.reshape(flat),
             degrees.reshape((3,) + flat),
         )
+        smoothed, coarse = finish(ny, smoothed, blocks)
         coarse = jnp.transpose(coarse.reshape(CMODES**3, 4, 2, 128), (0, 2, 1, 3))
         return smoothed.reshape(right_side.shape), coarse.reshape(CMODES**3, 2, 512)
 

time: 38.2 us -> 37.8 us (0.990)
  local copies, waits for them, and re-layouts: 1.79 us -> 0 us
  Pallas kernels: 35.6 us -> 37 us
    pallas_call x0 -> x1, Pallas kernels: none -> 1.8 us  [finish(): pl.pallas_call(functools.partial(finish_kernel, ny), out_shape=(jax.Shape...]
    unnamed x2 -> x0, local copies, waits for them, and re-layouts: 1.79 us -> none
    pallas_call x1, Pallas kernels: 35.6 us -> 35.2 us  [smoother(): pl.pallas_call(functools.partial(kernel, nx, ny), out_shape=(jax.ShapeDty...]
where the time goes in v3:
time: 37.8 us; the launch traced here: 37.6 us
  Pallas kernels  37 us (98%)
  between operations  0.64 us (2%)
    pallas_call x1, Pallas kernels, smoother(): pl.pallas_call(functools.partial(kernel, nx, ny), out_shape=(jax.ShapeDty...  35.2 us
    pallas_call x1, Pallas kernels, finish(): pl.pallas_call(functools.partial(finish_kernel, ny), out_shape=(jax.Shape...  1.8 us

profile of v3, /device:TPU:17, one launch (start us, length us, event | category | flops | bytes accessed | tf_op | source)
XLA Modules:
  0.0 37.6 jit_solution(1065330702021904425)
XLA Ops:
  0.6 35.2 %shard_map.50 = (f32[7,7,7,8,128]{4,3,2,1,0:T(8,128)S(1)}, f32[128,512]{1,0:T(8,128)S(1)}) custom-call(f32[7,7,7,8,128]{4,3,2,1,0:T(8,128)} %bitcast.9, f32[8,128]{1,0:T(8,128)} %bitcast.11, s32[3,8,128]{2,1,0:T(8,128)} %bitcast.10), custom_call_target="tpu_custom_call" | custom-call | tf_op jit(solution)/shard_map/pallas_call | solution.py:419
  35.8 1.8 %shard_map.51 = (f32[7,7,7,8,128]{4,3,2,1,0:T(8,128)}, f32[512,128]{1,0:T(8,128)}) custom-call(f32[7,7,7,8,128]{4,3,2,1,0:T(8,128)S(1)} %get-tuple-element.6.u, f32[128,512]{1,0:T(8,128)S(1)} %get-tuple-element.7.blocks), custom_call_target="tpu_custom_call" | custom-call | tf_op jit(solution)/shard_map/pallas_call | solution.py:481
